TPU v7x, 512 devices: a whole 4x4x16 slice. The times are simulated.
512 devices in a mesh: lat: 16 (over z_lo, core), lon: 32 (over x, y, z_hi).
Axes of the slice: x: 4, y: 4, z: 16 (z_hi: 2, z_lo: 8; z = z_hi * 8 + z_lo), core: 2. Of those that a mesh axis runs over, the one named last changes fastest.
Arguments:
- queries: bfloat16 [128, 512, 512], P('lat', 'lon'), may hold values from -180 to 180
- key_cells: bfloat16 [128, 512, 512], P('lat', 'lon'), may hold values from -15 to 15
- value_cells: bfloat16 [128, 512, 512], P('lat', 'lon'), may hold values from -5 to 5
- grad_output: bfloat16 [128, 512, 512], P('lat', 'lon'), may hold values from -5 to 5
- rel_bias: float32 [8, 169], replicated, may hold values from -4 to 4
Outputs:
- output: bfloat16 [128, 512, 512], P('lat', 'lon')
- grad_query: bfloat16 [128, 512, 512], P('lat', 'lon')
- grad_key: bfloat16 [128, 512, 512], P('lat', 'lon')
- grad_value: bfloat16 [128, 512, 512], P('lat', 'lon')
All inputs are finite; a program needn't handle non-finite values.
Results may differ from a plain program's by a relative error of at most 0.009.
Values may be sent and summed in bfloat16 or wider, within the bound.
A program may use at most 64 MiB of HBM per device.

v0:
```python
import jax
import jax.numpy as jnp
from jax import lax
from jax.sharding import PartitionSpec as P

HEAD_DIM = 64
TILE = 8
RADIUS = 6


HIGH = lax.Precision.HIGHEST


def padded_2(block, sides, width):
    for axis, dim in sides:
        count = lax.axis_size(axis)
        forward = [(i, i + 1) for i in range(count - 1)]
        forward.append((count - 1, 0))
        backward = [(target, source) for source, target in forward]
        low = lax.ppermute(
            lax.slice_in_dim(block, block.shape[dim] - width, None, axis=dim), axis, forward
        )
        high = lax.ppermute(lax.slice_in_dim(block, 0, width, axis=dim), axis, backward)
        block = jnp.concatenate([low, block, high], axis=dim)
    return block


def shifted(shard, axis, by):
    count = lax.axis_size(axis)
    return lax.ppermute(shard, axis, [(i, (i + by) % count) for i in range(count)])


def from_behind(value, axis, steps):
    count = lax.axis_size(axis)
    leading, last = (max(0, -steps), min(count, count - steps))
    return lax.ppermute(value, axis, [(source, source + steps) for source in range(leading, last)])


def offset_onehot(inner_len, outer_len, span_len, direction, offset):
    shape_all = (inner_len, outer_len, span_len)
    offset_index = lax.broadcasted_iota(jnp.int32, shape_all, 2)
    inner_index = lax.broadcasted_iota(jnp.int32, shape_all, 0)
    outer_index = lax.broadcasted_iota(jnp.int32, shape_all, 1)
    return (offset_index == direction * (outer_index - inner_index) + offset).astype(jnp.float32)


def expand_bias(rel_bias, direction, offset):
    span_len = 2 * RADIUS + 1
    extent = TILE + 2 * RADIUS
    head_count = rel_bias.shape[0]
    offsets_table = rel_bias.reshape(head_count, span_len, span_len)
    onehot = offset_onehot(TILE, extent, span_len, direction, offset)
    partial_sum = jnp.einsum("hab,jcb->hajc", offsets_table, onehot, precision=HIGH)
    expanded = jnp.einsum("ira,hajc->hijrc", onehot, partial_sum, precision=HIGH)
    inside = jnp.einsum("ira,jcb->ijrc", onehot, onehot, precision=HIGH) > 0.5
    return (
        expanded.reshape(head_count, TILE * TILE, extent * extent),
        inside.reshape(TILE * TILE, extent * extent),
    )


def to_tiles(values):
    height, breadth, channels = values.shape
    arranged = values.reshape(height // TILE, TILE, breadth // TILE, TILE, channels).transpose(
        0, 2, 1, 3, 4
    )
    return arranged.reshape(-1, TILE * TILE, channels)


def from_tiles(tiled, height, breadth):
    channels = tiled.shape[-1]
    arranged = tiled.reshape(height // TILE, breadth // TILE, TILE, TILE, channels).transpose(
        0, 2, 1, 3, 4
    )
    return arranged.reshape(height, breadth, channels)


def neighbourhoods(padded, breadth):
    extent = TILE + 2 * RADIUS
    pieces = []
    for col_tile in range(breadth // TILE):
        pieces.append(padded[0:extent, col_tile * TILE : col_tile * TILE + extent])
    stacked = jnp.stack(pieces)
    return stacked.reshape(len(pieces), extent * extent, padded.shape[-1])


def query_group(
    query_tiles, key_blocks, value_blocks, grad_tiles, bias_part, allowed, factor, group_size
):
    tile_count, query_len, span_cols = query_tiles.shape
    key_len = key_blocks.shape[1]
    head_size = span_cols // group_size
    query_heads = query_tiles.reshape(tile_count, query_len, group_size, head_size)
    grad_heads = grad_tiles.reshape(tile_count, query_len, group_size, head_size)
    key_heads = key_blocks.reshape(tile_count, key_len, group_size, head_size)
    value_heads = value_blocks.reshape(tile_count, key_len, group_size, head_size)
    scores = (
        jnp.einsum("tqhd,tkhd->thqk", query_heads, key_heads, preferred_element_type=jnp.float32)
        * factor
        + bias_part[None]
    )
    scores = jnp.where(allowed[:, None], scores, -jnp.inf)
    row_max = jnp.max(scores, axis=-1, keepdims=True)
    log_total = row_max + jnp.log(jnp.sum(jnp.exp(scores - row_max), axis=-1, keepdims=True))
    probability = jnp.exp(scores - log_total)
    weights = probability.astype(jnp.bfloat16)
    attended = jnp.einsum(
        "thqk,tkhd->tqhd", weights, value_heads, preferred_element_type=jnp.float32
    )
    row_dot = jnp.sum(grad_heads.astype(jnp.float32) * attended, axis=-1)
    grad_prob = jnp.einsum(
        "tqhd,tkhd->thqk", grad_heads, value_heads, preferred_element_type=jnp.float32
    )
    dscore = (probability * (grad_prob - jnp.transpose(row_dot, (0, 2, 1))[..., None])).astype(
        jnp.bfloat16
    )
    grad_q = (
        jnp.einsum("thqk,tkhd->tqhd", dscore, key_heads, preferred_element_type=jnp.float32)
        * factor
    )
    return (
        attended.reshape(tile_count, query_len, span_cols),
        grad_q.reshape(tile_count, query_len, span_cols),
        jnp.transpose(log_total[..., 0], (0, 2, 1)),
        row_dot,
        dscore,
        weights,
        query_heads,
        grad_heads,
    )


def shards(queries, key_cells, value_cells, grad_output, rel_bias):
    height, breadth, channels = queries.shape
    head_count = rel_bias.shape[0]
    group_size = 4
    group_cols = group_size * HEAD_DIM
    extent = TILE + 2 * RADIUS
    factor = HEAD_DIM ** (-0.5)
    lat_total = height * lax.axis_size("lat")
    lat_first = lax.axis_index("lat") * height
    grid_shape = (height // TILE, breadth // TILE, extent)
    tile_row = lax.broadcasted_iota(jnp.int32, grid_shape, 0)
    position = lax.broadcasted_iota(jnp.int32, grid_shape, 2)
    global_row = lat_first + tile_row * TILE - RADIUS + position
    row_inside = ((global_row >= 0) & (global_row < lat_total)).reshape(-1, extent, 1)
    cell_inside = jnp.broadcast_to(row_inside, (row_inside.shape[0], extent, extent)).reshape(
        -1, extent * extent
    )
    paired = jnp.stack([key_cells, value_cells])
    padded = padded_2(paired, (("lat", 1), ("lon", 2)), RADIUS)
    query_tiles = to_tiles(queries)
    grad_tiles = to_tiles(grad_output)
    bias_query, inside_query = expand_bias(rel_bias, 1, 0)
    allowed = inside_query[None] & cell_inside[:, None, :]
    collected = jnp.zeros((2, height + 2 * RADIUS, breadth + 2 * RADIUS, channels), jnp.float32)
    outputs, grads_q, totals, dots = ([], [], [], [])
    for group in range(head_count // group_size):
        start_col = group * group_cols
        key_blocks = neighbourhoods(padded[0, :, :, start_col : start_col + group_cols], breadth)
        value_blocks = neighbourhoods(padded[1, :, :, start_col : start_col + group_cols], breadth)
        results = query_group(
            query_tiles[:, :, start_col : start_col + group_cols],
            key_blocks,
            value_blocks,
            grad_tiles[:, :, start_col : start_col + group_cols],
            bias_query[group * group_size : (group + 1) * group_size],
            allowed,
            factor,
            group_size,
        )
        attended, grad_q, log_total, row_dot, dscore, weights, query_heads, grad_heads = results
        outputs.append(attended.astype(jnp.bfloat16))
        grads_q.append(grad_q.astype(jnp.bfloat16))
        totals.append(log_total)
        dots.append(row_dot)
        grad_k = (
            jnp.einsum("thqk,tqhd->tkhd", dscore, query_heads, preferred_element_type=jnp.float32)
            * factor
        )
        grad_v = jnp.einsum(
            "thqk,tqhd->tkhd", weights, grad_heads, preferred_element_type=jnp.float32
        )
        both_terms = jnp.stack([grad_k, grad_v]).reshape(
            2, grad_k.shape[0], extent, extent, group_cols
        )
        index = 0
        for col_tile in range(breadth // TILE):
            row_start = 0
            col_start = col_tile * TILE
            collected = collected.at[
                :,
                row_start : row_start + extent,
                col_start : col_start + extent,
                start_col : start_col + group_cols,
            ].add(both_terms[:, index])
            index = index + 1
    output = from_tiles(jnp.concatenate(outputs, axis=-1), height, breadth)
    grad_query = from_tiles(jnp.concatenate(grads_q, axis=-1), height, breadth)
    westward = shifted(collected[:, :, :RADIUS], "lon", -1)
    eastward = shifted(collected[:, :, breadth + RADIUS :], "lon", 1)
    collected = collected[:, :, RADIUS : breadth + RADIUS]
    collected = collected.at[:, :, breadth - RADIUS :].add(westward)
    collected = collected.at[:, :, :RADIUS].add(eastward)
    northward = from_behind(collected[:, :RADIUS], "lat", -1)
    southward = from_behind(collected[:, height + RADIUS :], "lat", 1)
    collected = collected[:, RADIUS : height + RADIUS]
    collected = collected.at[:, height - RADIUS :].add(northward)
    collected = collected.at[:, :RADIUS].add(southward)
    grad_key = collected[0].astype(jnp.bfloat16)
    grad_value = collected[1].astype(jnp.bfloat16)
    return (output, grad_query, grad_key, grad_value)


def solution(mesh):
    in_specs = (
        P("lat", "lon", None),
        P("lat", "lon", None),
        P("lat", "lon", None),
        P("lat", "lon", None),
        P(),
    )
    out_specs = (
        P("lat", "lon", None),
        P("lat", "lon", None),
        P("lat", "lon", None),
        P("lat", "lon", None),
    )
    return jax.shard_map(shards, mesh=mesh, in_specs=in_specs, out_specs=out_specs, check_vma=False)
```

profile of v0, /device:TPU:72, one launch (start us, length us, event | category | flops | bytes accessed | tf_op | source)
XLA Modules:
  0.0 276.0 jit_solution(10975244552288097151)
XLA Ops:
  0.6 1.1 fusion.31
  1.8 1.9 collective-permute-start.1
  3.7 2.4 collective-permute-start
  8.0 2.8 convolution_bitcast_fusion
  10.8 3.0 %fusion.49 = (f32[4,8,8,20,20]{3,4,1,2,0:T(8,128)}, f32[4,8,8,20,20]{3,4,1,2,0:T(8,128)}) fusion(f32[8,8,8,20,20]{3,4,1,2,0:T(8,128)S(1)} %convolution_bitcast_fusion), kind=kLoop, calls=%fused_computation.105 | loop fusion | bytes 1638400 | tf_op jit(solution)/shard_map/slice | solution.py:167
  17.7 13.8 %collective-permute-start.3 = (bf16[2,20,6,512]{3,2,1,0:T(8,128)(2,1)}, bf16[2,20,6,512]{3,2,1,0:T(8,128)(2,1)}, u32[]{:S(2)}, u32[]{:S(2)}) collective-permute-start(bf16[2,20,6,512]{3,2,1,0:T(8,128)(2,1)} %get-tuple-element.113), channel_id=1, source_target_pairs={{1,0},{2,1},{3,2},{4,3},{5,4},{6,5},{7,6},{8,7},{9,8},{10,9},{11,1... | collective-permute-start | bytes 737288 | tf_op jit(solution)/shard_map/ppermute | solution.py:23
  31.5 2.2 collective-permute-start.2
  34.5 3.2 %copy.138 = f32[4,8,8,20,20]{4,3,2,1,0:T(8,128)S(1)} copy(f32[4,8,8,20,20]{3,4,1,2,0:T(8,128)} %get-tuple-element.101) | data formatting | bytes 819200 | tf_op jit(solution)/shard_map/slice | solution.py:167
  37.7 1.5 add.109
  40.1 1.8 and.54
  42.9 3.2 %copy.131 = f32[4,8,8,20,20]{4,3,2,1,0:T(8,128)S(1)} copy(f32[4,8,8,20,20]{3,4,1,2,0:T(8,128)} %get-tuple-element.100) | data formatting | bytes 819200 | tf_op jit(solution)/shard_map/slice | solution.py:167
  46.1 1.5 add.105
  49.4 1.5 collective-permute-done.3
  50.8 20.1 %collective-permute-done.2 = bf16[2,20,6,512]{3,2,1,0:T(8,128)(2,1)} collective-permute-done((bf16[2,20,6,512]{3,2,1,0:T(8,128)(2,1)}, bf16[2,20,6,512]{3,2,1,0:T(8,128)(2,1)}, u32[]{:S(2)}, u32[]{:S(2)}) %collective-permute-start.2) | collective-permute-done | bytes 245792 | tf_op jit(solution)/shard_map/ppermute | solution.py:20
  70.9 1.9 pad_maximum_fusion
  76.8 1.3 stack.67
  81.1 1.4 convolution_bitcast_fusion.1
  82.5 1.1 multiply_reduce_fusion
  83.6 1.2 fusion.13
  86.0 1.1 multiply_reduce_fusion.1
  88.3 1.3 fusion.1
  89.6 2.1 copy.150
  91.7 2.1 stack.78
  93.8 2.3 constant_dynamic-update-slice_fusion.1
  97.1 2.1 stack.79
  99.2 1.5 constant_dynamic-update-slice_fusion
  100.7 2.2 fusion.51
  102.9 1.5 copy.180
  105.6 1.5 reshape.499
  107.1 2.0 copy.165
  109.1 2.4 reshape.500
  111.5 2.3 scatter-add.26
  114.9 3.7 %add_select_fusion = f32[2,20,20,256]{3,0,2,1:T(2,128)} fusion(f32[1,2,20,20,256]{4,0,3,2,1:T(1,128)S(1)} %reshape.499, f32[1,2,20,20,256]{4,0,3,2,1:T(1,128)S(1)} %copy-done.3, f32[2,20,28,512]{3,0,2,1:T(2,128)S(1)} %fusion.25, s32[]{:T(128)} %bitcast.41, s32[]{:T(128)} %bitcast.42, pred[]{:T(512)} %and_reduce_fusion), kind=kLoop, calls=%fused_computation.27 | loop fusion | flops 614400 | bytes 3276809 | tf_op jit(solution)/shard_map/select.10
  118.6 17.5 %scatter-add.30 = f32[2,20,28,512]{3,0,2,1:T(2,128)S(1)} dynamic-update-slice(f32[2,20,28,512]{3,0,2,1:T(2,128)S(1)} %fusion.25, f32[2,20,20,256]{3,0,2,1:T(2,128)} %add_select_fusion, s32[]{:T(128)} %constant.240.clone.1, s32[]{:T(128)} %constant.240.clone.1, s32[]{:T(128)} %bitcast.41, s32[]{:T(128)} %bitcast.42) | dynamic-update-slice | bytes 1638404 | tf_op jit(solution)/shard_map/scatter-add | solution.py:196
  136.1 2.0 fusion.24
  138.2 1.3 fusion.50
  139.5 35.4 %collective-permute-start.4 = (f32[2,20,6,512]{3,0,2,1:T(2,128)}, f32[2,20,6,512]{3,0,2,1:T(2,128)}, u32[]{:S(2)}, u32[]{:S(2)}) collective-permute-start(f32[2,20,6,512]{3,0,2,1:T(2,128)} %get-tuple-element.103), channel_id=1, source_target_pairs={{0,31},{1,0},{2,1},{3,2},{4,3},{5,4},{6,5},{7,6},{8,7},{9,8},{10,9... | collective-permute-start | bytes 1474568 | tf_op jit(solution)/shard_map/ppermute | solution.py:30
  174.9 1.5 slice.429
  177.7 1.0 copy.132
  179.5 1.9 collective-permute-start.5
  182.4 48.8 %collective-permute-done.4 = f32[2,20,6,512]{3,0,2,1:T(2,128)} collective-permute-done((f32[2,20,6,512]{3,0,2,1:T(2,128)}, f32[2,20,6,512]{3,0,2,1:T(2,128)}, u32[]{:S(2)}, u32[]{:S(2)}) %collective-permute-start.4) | collective-permute-done | bytes 491552 | tf_op jit(solution)/shard_map/ppermute | solution.py:30
  231.2 2.1 fusion.28
  233.3 25.5 %collective-permute-done.5 = f32[2,20,6,512]{3,0,2,1:T(2,128)S(1)} collective-permute-done((f32[2,20,6,512]{3,0,2,1:T(2,128)}, f32[2,20,6,512]{3,0,2,1:T(2,128)S(1)}, u32[]{:S(2)}, u32[]{:S(2)}) %collective-permute-start.5) | collective-permute-done | bytes 491552 | tf_op jit(solution)/shard_map/ppermute | solution.py:30
  258.8 2.1 fusion.27
  260.9 1.5 fusion.52
  262.4 1.9 collective-permute-start.6
  264.6 2.4 collective-permute-start.7
  269.8 3.9 %collective-permute-done.7 = f32[2,6,16,512]{3,0,2,1:T(2,128)S(1)} collective-permute-done((f32[2,6,16,512]{3,0,2,1:T(2,128)S(1)}, f32[2,6,16,512]{3,0,2,1:T(2,128)S(1)}, u32[]{:S(2)}, u32[]{:S(2)}) %collective-permute-start.7) | collective-permute-done | bytes 393248 | tf_op jit(solution)/shard_map/ppermute | solution.py:36
  (138 shorter events, 30.5 us)
Async XLA Ops:
  0.6 5.5 %copy-start = (bf16[8,16,512]{2,1,0:T(8,128)(2,1)S(1)}, bf16[8,16,512]{2,1,0:T(8,128)(2,1)}, u32[]{:S(2)}) copy-start(bf16[8,16,512]{2,1,0:T(8,128)(2,1)} %param.24) | copy-start | bytes 393220
  1.8 14.9 %collective-permute-start.1 = (bf16[2,6,16,512]{3,2,1,0:T(8,128)(2,1)S(1)}, bf16[2,6,16,512]{3,2,1,0:T(8,128)(2,1)S(1)}, u32[]{:S(2)}, u32[]{:S(2)}) collective-permute-start(bf16[2,6,16,512]{3,2,1,0:T(8,128)(2,1)S(1)} %get-tuple-element.129), channel_id=1, source_target_pairs={{32,0},{64,32},{96,64},{128,96},{160,128},{192,160},{224,192},{256... | collective-permute-start | bytes 589832 | tf_op jit(solution)/shard_map/ppermute | solution.py:23
  3.7 13.0 %collective-permute-start = (bf16[2,6,16,512]{3,2,1,0:T(8,128)(2,1)S(1)}, bf16[2,6,16,512]{3,2,1,0:T(8,128)(2,1)S(1)}, u32[]{:S(2)}, u32[]{:S(2)}) collective-permute-start(bf16[2,6,16,512]{3,2,1,0:T(8,128)(2,1)S(1)} %get-tuple-element.128), channel_id=1, source_target_pairs={{0,32},{32,64},{64,96},{96,128},{128,160},{160,192},{192,224},{224... | collective-permute-start | bytes 589832 | tf_op jit(solution)/shard_map/ppermute | solution.py:20
  10.7 3.1 %copy-start.30 = (bf16[8,16,512]{2,1,0:T(8,128)(2,1)S(1)}, bf16[8,16,512]{2,1,0:T(8,128)(2,1)}, u32[]{:S(2)}) copy-start(bf16[8,16,512]{2,1,0:T(8,128)(2,1)} %param.21) | copy-start | bytes 393220
  10.7 4.6 %copy-start.32 = (s32[4]{0:T(128)S(1)}, s32[4]{0:T(128)}, u32[]{:S(2)}) copy-start(s32[4]{0:T(128)} %constant.246.clone.1) | copy-start | bytes 52
  10.7 5.9 %copy-start.12 = (bf16[8,16,512]{2,1,0:T(8,128)(2,1)S(1)}, bf16[8,16,512]{2,1,0:T(8,128)(2,1)}, u32[]{:S(2)}) copy-start(bf16[8,16,512]{2,1,0:T(8,128)(2,1)} %param.22) | copy-start | bytes 393220
  10.8 5.9 %copy-start.13 = (bf16[8,16,512]{2,1,0:T(8,128)(2,1)S(1)}, bf16[8,16,512]{2,1,0:T(8,128)(2,1)}, u32[]{:S(2)}) copy-start(bf16[8,16,512]{2,1,0:T(8,128)(2,1)} %param.23) | copy-start | bytes 393220
  16.6 17.9 %copy-start.27 = (bf16[2,6,16,512]{3,2,1,0:T(8,128)(2,1)}, bf16[2,6,16,512]{3,2,1,0:T(8,128)(2,1)S(1)}, u32[]{:S(2)}) copy-start(bf16[2,6,16,512]{3,2,1,0:T(8,128)(2,1)S(1)} %collective-permute-done.1) | copy-start | bytes 589828
  16.7 17.8 %copy-start.28 = (bf16[2,6,16,512]{3,2,1,0:T(8,128)(2,1)}, bf16[2,6,16,512]{3,2,1,0:T(8,128)(2,1)S(1)}, u32[]{:S(2)}) copy-start(bf16[2,6,16,512]{3,2,1,0:T(8,128)(2,1)S(1)} %collective-permute-done) | copy-start | bytes 589828
  17.7 33.1 %collective-permute-start.3 = (bf16[2,20,6,512]{3,2,1,0:T(8,128)(2,1)}, bf16[2,20,6,512]{3,2,1,0:T(8,128)(2,1)}, u32[]{:S(2)}, u32[]{:S(2)}) collective-permute-start(bf16[2,20,6,512]{3,2,1,0:T(8,128)(2,1)} %get-tuple-element.113), channel_id=1, source_target_pairs={{1,0},{2,1},{3,2},{4,3},{5,4},{6,5},{7,6},{8,7},{9,8},{10,9},{11,1... | collective-permute-start | bytes 737288 | tf_op jit(solution)/shard_map/ppermute | solution.py:23
  31.5 39.4 %collective-permute-start.2 = (bf16[2,20,6,512]{3,2,1,0:T(8,128)(2,1)}, bf16[2,20,6,512]{3,2,1,0:T(8,128)(2,1)}, u32[]{:S(2)}, u32[]{:S(2)}) collective-permute-start(bf16[2,20,6,512]{3,2,1,0:T(8,128)(2,1)} %get-tuple-element.112), channel_id=1, source_target_pairs={{0,1},{1,2},{2,3},{3,4},{4,5},{5,6},{6,7},{7,8},{8,9},{9,10},{10,1... | collective-permute-start | bytes 737288 | tf_op jit(solution)/shard_map/ppermute | solution.py:20
  73.5 6.8 %copy-start.19 = (bf16[1,400,4,64]{1,3,2,0:T(8,128)(2,1)}, bf16[1,400,4,64]{1,3,2,0:T(8,128)(2,1)S(1)}, u32[]{:S(2)}) copy-start(bf16[1,400,4,64]{1,3,2,0:T(8,128)(2,1)S(1)} %copy.136) | copy-start | bytes 614404
  74.0 6.3 %copy-start.23 = (bf16[1,400,4,64]{1,3,2,0:T(8,128)(2,1)}, bf16[1,400,4,64]{1,3,2,0:T(8,128)(2,1)S(1)}, u32[]{:S(2)}) copy-start(bf16[1,400,4,64]{1,3,2,0:T(8,128)(2,1)S(1)} %copy.135) | copy-start | bytes 614404
  76.0 4.3 %copy-start.11 = (f32[4,64,400]{2,1,0:T(8,128)S(1)}, f32[4,64,400]{2,1,0:T(8,128)}, u32[]{:S(2)}) copy-start(f32[4,64,400]{2,1,0:T(8,128)} %add.109) | copy-start | bytes 1228804
  76.0 4.3 %copy-start.15 = (bf16[2,64,256]{1,2,0:T(8,128)(2,1)S(1)}, bf16[2,64,256]{1,2,0:T(8,128)(2,1)}, u32[]{:S(2)}) copy-start(bf16[2,64,256]{1,2,0:T(8,128)(2,1)} %copy.171) | copy-start | bytes 196612
  76.3 8.5 %copy-start.17 = (bf16[1,400,4,64]{1,3,2,0:T(8,128)(2,1)}, bf16[1,400,4,64]{1,3,2,0:T(8,128)(2,1)S(1)}, u32[]{:S(2)}) copy-start(bf16[1,400,4,64]{1,3,2,0:T(8,128)(2,1)S(1)} %copy.128) | copy-start | bytes 614404
  76.8 8.0 %copy-start.21 = (bf16[1,400,4,64]{1,3,2,0:T(8,128)(2,1)}, bf16[1,400,4,64]{1,3,2,0:T(8,128)(2,1)S(1)}, u32[]{:S(2)}) copy-start(bf16[1,400,4,64]{1,3,2,0:T(8,128)(2,1)S(1)} %copy.127) | copy-start | bytes 614404
  79.1 2.0 copy-start.14
  82.5 2.3 copy-start.10
  84.8 1.2 copy-start.25
  84.8 1.2 copy-start.26
  87.5 0.8 copy-start.6
  97.1 2.2 copy-start.4
  100.7 3.8 %copy-start.8 = (bf16[2,4,64,400]{3,2,1,0:T(8,128)(2,1)S(1)}, bf16[2,4,64,400]{3,2,1,0:T(8,128)(2,1)}, u32[]{:S(2)}) copy-start(bf16[2,4,64,400]{3,2,1,0:T(8,128)(2,1)} %fusion.13) | copy-start | bytes 1228804
  100.7 3.7 %copy-start.16 = (bf16[2,64,256]{1,2,0:T(8,128)(2,1)S(1)}, bf16[2,64,256]{1,2,0:T(8,128)(2,1)}, u32[]{:S(2)}) copy-start(bf16[2,64,256]{1,2,0:T(8,128)(2,1)} %copy.171) | copy-start | bytes 196612
  111.5 2.3 copy-start.5
  111.5 3.4 %copy-start.3 = (f32[1,2,20,20,256]{4,0,3,2,1:T(1,128)S(1)}, f32[1,2,20,20,256]{4,0,3,2,1:T(1,128)}, u32[]{:S(2)}) copy-start(f32[1,2,20,20,256]{4,0,3,2,1:T(1,128)} %reshape.500) | copy-start | bytes 2457604
  138.2 43.2 %copy-start.9 = (bf16[2,4,64,400]{3,2,1,0:T(8,128)(2,1)S(1)}, bf16[2,4,64,400]{3,2,1,0:T(8,128)(2,1)}, u32[]{:S(2)}) copy-start(bf16[2,4,64,400]{3,2,1,0:T(8,128)(2,1)} %fusion.13) | copy-start | bytes 1228804
  138.2 43.2 %copy-start.20 = (bf16[1,400,4,64]{1,3,2,0:T(8,128)(2,1)S(1)}, bf16[1,400,4,64]{1,3,2,0:T(8,128)(2,1)}, u32[]{:S(2)}) copy-start(bf16[1,400,4,64]{1,3,2,0:T(8,128)(2,1)} %copy-done.19) | copy-start | bytes 614404
  138.2 43.2 %copy-start.24 = (bf16[1,400,4,64]{1,3,2,0:T(8,128)(2,1)S(1)}, bf16[1,400,4,64]{1,3,2,0:T(8,128)(2,1)}, u32[]{:S(2)}) copy-start(bf16[1,400,4,64]{1,3,2,0:T(8,128)(2,1)} %copy-done.23) | copy-start | bytes 614404
  139.5 91.7 %collective-permute-start.4 = (f32[2,20,6,512]{3,0,2,1:T(2,128)}, f32[2,20,6,512]{3,0,2,1:T(2,128)}, u32[]{:S(2)}, u32[]{:S(2)}) collective-permute-start(f32[2,20,6,512]{3,0,2,1:T(2,128)} %get-tuple-element.103), channel_id=1, source_target_pairs={{0,31},{1,0},{2,1},{3,2},{4,3},{5,4},{6,5},{7,6},{8,7},{9,8},{10,9... | collective-permute-start | bytes 1474568 | tf_op jit(solution)/shard_map/ppermute | solution.py:30
  179.5 79.3 %collective-permute-start.5 = (f32[2,20,6,512]{3,0,2,1:T(2,128)}, f32[2,20,6,512]{3,0,2,1:T(2,128)S(1)}, u32[]{:S(2)}, u32[]{:S(2)}) collective-permute-start(f32[2,20,6,512]{3,0,2,1:T(2,128)} %get-tuple-element.102), channel_id=1, source_target_pairs={{0,1},{1,2},{2,3},{3,4},{4,5},{5,6},{6,7},{7,8},{8,9},{9,10},{10,1... | collective-permute-start | bytes 1474568 | tf_op jit(solution)/shard_map/ppermute | solution.py:30
  182.4 81.9 %copy-start.7 = (bf16[2,4,64,400]{3,2,1,0:T(8,128)(2,1)S(1)}, bf16[2,4,64,400]{3,2,1,0:T(8,128)(2,1)}, u32[]{:S(2)}) copy-start(bf16[2,4,64,400]{3,2,1,0:T(8,128)(2,1)} %copy-done.6) | copy-start | bytes 1228804
  182.4 81.9 %copy-start.18 = (bf16[1,400,4,64]{1,3,2,0:T(8,128)(2,1)S(1)}, bf16[1,400,4,64]{1,3,2,0:T(8,128)(2,1)}, u32[]{:S(2)}) copy-start(bf16[1,400,4,64]{1,3,2,0:T(8,128)(2,1)} %copy-done.17) | copy-start | bytes 614404
  182.4 82.0 %copy-start.22 = (bf16[1,400,4,64]{1,3,2,0:T(8,128)(2,1)S(1)}, bf16[1,400,4,64]{1,3,2,0:T(8,128)(2,1)}, u32[]{:S(2)}) copy-start(bf16[1,400,4,64]{1,3,2,0:T(8,128)(2,1)} %copy-done.21) | copy-start | bytes 614404
  233.3 33.7 %copy-start.29 = (bf16[1,2,8,8,256]{4,3,2,1,0:T(8,128)(2,1)S(1)}, bf16[1,2,8,8,256]{4,3,2,1,0:T(8,128)(2,1)}, u32[]{:S(2)}) copy-start(bf16[1,2,8,8,256]{4,3,2,1,0:T(8,128)(2,1)} %convert_element_type.90) | copy-start | bytes 196612
  233.3 34.4 %copy-start.31 = (bf16[2,64,4,64]{1,3,2,0:T(8,128)(2,1)S(1)}, bf16[2,64,4,64]{1,3,2,0:T(8,128)(2,1)}, u32[]{:S(2)}) copy-start(bf16[2,64,4,64]{1,3,2,0:T(8,128)(2,1)} %fusion.16) | copy-start | bytes 196612
  260.9 8.1 %copy-start.2 = (f32[2,20,16,512]{3,0,2,1:T(2,128)S(1)}, f32[2,20,16,512]{3,0,2,1:T(2,128)}, u32[]{:S(2)}) copy-start(f32[2,20,16,512]{3,0,2,1:T(2,128)} %fusion.27) | copy-start | bytes 3932164
  262.4 7.2 %collective-permute-start.6 = (f32[2,6,16,512]{3,0,2,1:T(2,128)S(1)}, f32[2,6,16,512]{3,0,2,1:T(2,128)S(1)}, u32[]{:S(2)}, u32[]{:S(2)}) collective-permute-start(f32[2,6,16,512]{3,0,2,1:T(2,128)S(1)} %get-tuple-element.107), channel_id=1, source_target_pairs={{32,0},{64,32},{96,64},{128,96},{160,128},{192,160},{224,192},{256... | collective-permute-start | bytes 1179656 | tf_op jit(solution)/shard_map/ppermute | solution.py:36
  264.6 9.1 %collective-permute-start.7 = (f32[2,6,16,512]{3,0,2,1:T(2,128)S(1)}, f32[2,6,16,512]{3,0,2,1:T(2,128)S(1)}, u32[]{:S(2)}, u32[]{:S(2)}) collective-permute-start(f32[2,6,16,512]{3,0,2,1:T(2,128)S(1)} %get-tuple-element.106), channel_id=1, source_target_pairs={{0,32},{32,64},{64,96},{96,128},{128,160},{160,192},{192,224},{224... | collective-permute-start | bytes 1179656 | tf_op jit(solution)/shard_map/ppermute | solution.py:36
  269.0 7.0 %copy-start.1 = (bf16[8,16,512]{2,1,0:T(8,128)(2,1)S(1)}, bf16[8,16,512]{2,1,0:T(8,128)(2,1)}, u32[]{:S(2)}) copy-start(bf16[8,16,512]{2,1,0:T(8,128)(2,1)} %param.24) | copy-start | bytes 393220
where the time goes:
time: 277 us; the launch traced here: 276 us
  waiting for transfers between devices  100 us (36%)
  local copies, waits for them, and re-layouts  80.9 us (29%)
  starting transfers between devices  62 us (22%)
  other arithmetic  19.1 us (7%)
  matrix products  12.3 us (4%)
    ppermute x2, waiting for transfers between devices, shifted(): lax.ppermute(shard, axis, [(i, (i + by) % count) for i in range(count)])  74.3 us
    ppermute x2, starting transfers between devices, shifted(): lax.ppermute(shard, axis, [(i, (i + by) % count) for i in range(count)])  37.3 us
    ppermute x2, waiting for transfers between devices, padded_2(): lax.ppermute(lax.slice_in_dim(block, block.shape[dim] - width, None, axis...  20.1 us
    scatter-add x2, local copies, waits for them, and re-layouts, shards(): collected = collected.at[:, row_start:row_start + extent, col_start:col_s...  19.9 us
    ppermute x2, starting transfers between devices, padded_2(): lax.ppermute(lax.slice_in_dim(block, 0, width, axis=dim), axis, backward)  15.7 us
    another operation x7, local copies, waits for them, and re-layouts, shards(): jnp.stack([grad_k, grad_v])  12.5 us
    slice x3, local copies, waits for them, and re-layouts, shards(): bias_query[group * group_size:(group + 1) * group_size]  9.39 us
    another operation x16, local copies, waits for them, and re-layouts, neighbourhoods(): stacked = jnp.stack(pieces)  6.33 us
  transfers between devices with their start and end apart: 8, of which 6 were waited for; matrix products, arithmetic and copies ran while one was open for 13% of the time, Pallas kernels for 0%

commit v1 on v0

v1 whole, which is shorter than its diff:
```python
import jax
import jax.numpy as jnp
from jax import lax
from jax.experimental import pallas as pl
from jax.experimental.pallas import tpu as pltpu
from jax.sharding import PartitionSpec as P

HEAD_DIM = 64
RADIUS = 6
SPAN = 13
MESH = pl.DeviceIdType.MESH
NEG = -1e30

CHUNKS = 4
HEIGHT = 8
BREADTH = 16
SIDE = 48
WEST = 96
EAST = 144
CENTRE = 224
STRIP = 192
NORTH = CENTRE
SOUTH = CENTRE + STRIP
KEYS = CENTRE + 2 * STRIP
ROW_AT = [0, 16, 32, 48, 64, 80, 192, 208]


def side_groups(base, kind):
    return [(base + t, base + 6 + t // 3, kind + t % 3) for t in range(6)]


def row_groups(base, rows):
    return [(base + r, base + r, kind) for r in rows for kind in (0, 1)]


def key_groups():
    def sides(base):
        return side_groups(base, 2) + side_groups(base, 5)

    centre = row_groups(0, range(6)) + sides(0) + row_groups(0, (6, 7))
    north = row_groups(-8, range(2, 6)) + sides(-8) + row_groups(-8, (6, 7))
    south = row_groups(8, range(6)) + sides(8)
    return [(g, 0) for g in centre] + [(g, 1) for g in north] + [(g, 2) for g in south]


def slot_iota():
    return lax.broadcasted_iota(jnp.int32, (8, 128), 0)


def offset_index(kind):
    slot = slot_iota()
    lane = lax.broadcasted_iota(jnp.int32, (8, 128), 1)
    row, col = lane // BREADTH, lane % BREADTH
    if kind < 2:
        cell = slot + 8 * kind
    else:
        first = -RADIUS if kind < 5 else BREADTH
        cell = jnp.where(slot < 6, first + slot, first + 2 * ((kind - 2) % 3) + slot - 6)
    f = cell - col + RADIUS
    return jnp.where((f >= 0) & (f < SPAN), (HEIGHT - 1 - row) * SPAN + f, 127)


def dot(a, b, on_a, on_b):
    return lax.dot_general(
        a, b, (((on_a,), (on_b,)), ((), ())), preferred_element_type=jnp.float32
    )


def kernel(
    q_ref, k_ref, v_ref, g_ref, rel_ref, o_ref, dq_ref, dk_ref, dv_ref,
    cells, edges, bias, table, padded, strips_out, strips_in, centre, sides_out, sides_in,
    lon_s, lon_r, lat_s, lat_r, rlat_s, rlat_r, rlon_s, rlon_r,
):
    lat, lon = lax.axis_index("lat"), lax.axis_index("lon")
    n_lat, n_lon = lax.axis_size("lat"), lax.axis_size("lon")
    west = (lat, lax.rem(lon + n_lon - 1, n_lon))
    east = (lat, lax.rem(lon + 1, n_lon))
    north = (lat - 1, lon)
    south = (lat + 1, lon)
    has_north, has_south = lat > 0, lat < n_lat - 1
    factor = HEAD_DIM**-0.5
    slot = slot_iota()

    barrier = pltpu.get_barrier_semaphore()
    for side in (west, east):
        pl.semaphore_signal(barrier, inc=1, device_id=side, device_id_type=MESH)

    @pl.when(has_north)
    def _():
        pl.semaphore_signal(barrier, inc=1, device_id=north, device_id_type=MESH)

    @pl.when(has_south)
    def _():
        pl.semaphore_signal(barrier, inc=1, device_id=south, device_id_type=MESH)

    def lanes(g):
        return pl.ds(128 * g, 128)

    for g in range(CHUNKS):
        for a, ref in ((0, k_ref), (1, v_ref)):
            block = ref[:, lanes(g)]
            cells[g, a, 0:96] = block[0:96]
            cells[g, a, 192:224] = block[96:128]
            wide = block.astype(jnp.float32)
            low = [wide[16 * r : 16 * r + 8] for r in range(8)]
            high = [wide[16 * r + 8 : 16 * r + 16] for r in range(8)]
            to_west, to_east = [], []
            for t in range(6):
                j, last = 2 * (t % 3), 6 + t // 3
                spare = low[last] if j == 6 else pltpu.roll(low[last], 6 - j, 0)
                to_west.append(jnp.where(slot < 6, low[t], spare))
                spare = high[last] if j == 4 else pltpu.roll(high[last], 4 - j, 0)
                to_east.append(jnp.where(slot < 6, pltpu.roll(high[t], 6, 0), spare))
            edges[g, 0, a] = jnp.concatenate(to_west, axis=0).astype(jnp.bfloat16)
            edges[g, 1, a] = jnp.concatenate(to_east, axis=0).astype(jnp.bfloat16)

    pl.semaphore_wait(barrier, 2 + has_north.astype(jnp.int32) + has_south.astype(jnp.int32))

    def remote(src, dst, sends, recvs, g, way, target):
        return pltpu.make_async_remote_copy(
            src_ref=src, dst_ref=dst, send_sem=sends.at[g, way], recv_sem=recvs.at[g, way],
            device_id=target, device_id_type=MESH,
        )

    def lon_copies(g):
        return [
            remote(edges.at[g, 0], cells.at[g, :, pl.ds(EAST, SIDE)], lon_s, lon_r, g, 0, west),
            remote(edges.at[g, 1], cells.at[g, :, pl.ds(WEST, SIDE)], lon_s, lon_r, g, 1, east),
        ]

    def lat_copies(g):
        up = remote(
            cells.at[g, :, pl.ds(0, STRIP)], cells.at[g, :, pl.ds(SOUTH, STRIP)], lat_s, lat_r, g, 0, north
        )
        down = remote(
            cells.at[g, :, pl.ds(32, STRIP)], cells.at[g, :, pl.ds(NORTH, STRIP)], lat_s, lat_r, g, 1, south
        )
        return up, down

    def back_lat_copies(g):
        up = remote(strips_out.at[g, 0], strips_in.at[g, 0], rlat_s, rlat_r, g, 0, north)
        down = remote(strips_out.at[g, 1], strips_in.at[g, 1], rlat_s, rlat_r, g, 1, south)
        return up, down

    def back_lon_copies(g):
        return [
            remote(sides_out.at[g, 0], sides_in.at[g, 0], rlon_s, rlon_r, g, 0, west),
            remote(sides_out.at[g, 1], sides_in.at[g, 1], rlon_s, rlon_r, g, 1, east),
        ]

    def start_pair(copies):
        up, down = copies

        @pl.when(has_north)
        def _():
            up.start()

        @pl.when(has_south)
        def _():
            down.start()

    def wait_pair(copies):
        up, down = copies

        @pl.when(has_south)
        def _():
            up.wait_recv()

        @pl.when(has_north)
        def _():
            down.wait_recv()

    for g in range(CHUNKS):
        for copy in lon_copies(g):
            copy.start()

    for g in range(CHUNKS):

        @pl.when(jnp.logical_not(has_north))
        def _():
            cells[g, :, NORTH : NORTH + STRIP] = jnp.zeros((2, STRIP, 128), jnp.bfloat16)

        @pl.when(jnp.logical_not(has_south))
        def _():
            cells[g, :, SOUTH : SOUTH + STRIP] = jnp.zeros((2, STRIP, 128), jnp.bfloat16)

    padded[...] = jnp.full(padded.shape, NEG, jnp.float32)
    padded[:, 128 : 128 + SPAN * SPAN] = rel_ref[...]
    line = padded[...]
    lane = lax.broadcasted_iota(jnp.int32, (8, 128), 1)
    for c in range(-8, 16):
        first = 128 + SPAN * (c - 1)
        rolled = pltpu.roll(line, 512 - first, 1)[:, :128]
        table[c + 8] = jnp.where(lane < 8 * SPAN, rolled, NEG)

    indices = [offset_index(kind) for kind in range(8)]
    outside = [
        None,
        jnp.where(has_north, 0.0, NEG).astype(jnp.float32),
        jnp.where(has_south, 0.0, NEG).astype(jnp.float32),
    ]

    def fill_bias(pair, carry):
        for half in range(2):
            head = 2 * pair + half
            rows = {}

            def row(c):
                if c not in rows:
                    rows[c] = jnp.broadcast_to(table[c + 8, pl.ds(head, 1), :], (8, 128))
                return rows[c]

            for i, ((c, spare, kind), region) in enumerate(key_groups()):
                source = row(c) if c == spare else jnp.where(slot < 6, row(c), row(spare))
                value = jnp.take_along_axis(source, indices[kind], axis=1)
                if outside[region] is not None:
                    value = value + outside[region]
                bias[pair, 8 * i : 8 * i + 8, 128 * half : 128 * half + 128] = value
        return carry

    lax.fori_loop(0, CHUNKS, fill_bias, 0)

    left = lax.broadcasted_iota(jnp.int32, (128, 128), 1) < HEAD_DIM
    top = lax.broadcasted_iota(jnp.int32, (128, 128), 0) < HEAD_DIM

    def by_head(block):
        wide = block.astype(jnp.float32)
        both = jnp.concatenate([jnp.where(left, wide, 0.0), jnp.where(left, 0.0, wide)], axis=0)
        return both.astype(jnp.bfloat16)

    def from_heads(found):
        return jnp.where(top, found[:, :128], found[:, 128:]).T

    def forward_strips(g):
        for copy in lon_copies(g):
            copy.wait_recv()
        start_pair(lat_copies(g))

    def attend(g):
        wait_pair(lat_copies(g))
        queries, grads = by_head(q_ref[:, lanes(g)]), by_head(g_ref[:, lanes(g)])
        keys, values = cells[g, 0], cells[g, 1]
        scores = dot(keys, queries, 1, 1) * factor + bias[g]
        row_max = jnp.max(scores, axis=0, keepdims=True)
        raised = jnp.exp(scores - row_max)
        probability = raised * (1.0 / jnp.sum(raised, axis=0, keepdims=True))
        weights = probability.astype(jnp.bfloat16)
        grad_prob = dot(values, grads, 1, 1)
        row_dot = jnp.sum(weights.astype(jnp.float32) * grad_prob, axis=0, keepdims=True)
        dscore = (probability * (grad_prob - row_dot)).astype(jnp.bfloat16)
        grad_v = dot(weights, grads, 1, 0)
        grad_k = dot(dscore, queries, 1, 0) * factor
        for a, found in ((0, grad_k), (1, grad_v)):
            strips_out[g, 0, a] = found[NORTH : NORTH + STRIP].astype(jnp.bfloat16)
            strips_out[g, 1, a] = found[SOUTH : SOUTH + STRIP].astype(jnp.bfloat16)
            centre[g, a] = found[:CENTRE]
        start_pair(back_lat_copies(g))
        o_ref[:, lanes(g)] = from_heads(dot(values, weights, 0, 0)).astype(jnp.bfloat16)
        grad_q = from_heads(dot(keys, dscore, 0, 0)) * factor
        dq_ref[:, lanes(g)] = grad_q.astype(jnp.bfloat16)

    def return_sides(g):
        wait_pair(back_lat_copies(g))

        @pl.when(has_south)
        def _():
            for a in range(2):
                centre[g, a, 32:224] += strips_in[g, 0, a].astype(jnp.float32)

        @pl.when(has_north)
        def _():
            for a in range(2):
                centre[g, a, 0:192] += strips_in[g, 1, a].astype(jnp.float32)

        for a in range(2):
            sides_out[g, 0, a] = centre[g, a, WEST : WEST + SIDE].astype(jnp.bfloat16)
            sides_out[g, 1, a] = centre[g, a, EAST : EAST + SIDE].astype(jnp.bfloat16)
        for copy in back_lon_copies(g):
            copy.start()

    def finish(g):
        for copy in back_lon_copies(g):
            copy.wait_recv()
        for a, ref in ((0, dk_ref), (1, dv_ref)):
            from_east = sides_in[g, 0, a].astype(jnp.float32)
            from_west = sides_in[g, 1, a].astype(jnp.float32)
            east_groups = [from_east[8 * t : 8 * t + 8] for t in range(6)]
            west_groups = [from_west[8 * t : 8 * t + 8] for t in range(6)]
            rows = []
            for r in range(8):
                if r < 6:
                    low, high = west_groups[r], pltpu.roll(east_groups[r], 2, 0)
                else:
                    w, e = west_groups[3 * (r - 6) :], east_groups[3 * (r - 6) :]
                    low = jnp.where(
                        slot < 2, pltpu.roll(w[0], 2, 0), jnp.where(slot < 4, pltpu.roll(w[1], 4, 0), pltpu.roll(w[2], 6, 0))
                    )
                    high = jnp.where(
                        slot < 4, pltpu.roll(e[0], 4, 0), jnp.where(slot < 6, pltpu.roll(e[1], 6, 0), e[2])
                    )
                at = ROW_AT[r]
                rows.append(centre[g, a, at : at + 8] + jnp.where(slot < 6, low, 0.0))
                rows.append(centre[g, a, at + 8 : at + 16] + jnp.where(slot >= 2, high, 0.0))
            ref[:, lanes(g)] = jnp.concatenate(rows, axis=0).astype(jnp.bfloat16)

    forward_strips(0)
    forward_strips(1)
    attend(0)
    forward_strips(2)
    return_sides(0)
    attend(1)
    forward_strips(3)
    return_sides(1)
    attend(2)
    return_sides(2)
    attend(3)
    return_sides(3)
    for g in range(CHUNKS):
        finish(g)

    for g in range(CHUNKS):
        for copy in lon_copies(g) + back_lon_copies(g):
            copy.wait_send()
        for up, down in (lat_copies(g), back_lat_copies(g)):

            @pl.when(has_north)
            def _():
                up.wait_send()

            @pl.when(has_south)
            def _():
                down.wait_send()


def shards(queries, key_cells, value_cells, grad_output, rel_bias):
    height, breadth, channels = queries.shape
    flat = [x.reshape(height * breadth, channels) for x in (queries, key_cells, value_cells, grad_output)]
    bf16, f32 = jnp.bfloat16, jnp.float32
    vmem = pl.BlockSpec(memory_space=pltpu.VMEM)
    semaphores = [pltpu.SemaphoreType.DMA((CHUNKS, 2))] * 8
    found = pl.pallas_call(
        kernel,
        out_shape=[jax.ShapeDtypeStruct((height * breadth, channels), bf16)] * 4,
        in_specs=[vmem] * 5,
        out_specs=[vmem] * 4,
        scratch_shapes=[
            pltpu.VMEM((CHUNKS, 2, KEYS, 128), bf16),
            pltpu.VMEM((CHUNKS, 2, 2, SIDE, 128), bf16),
            pltpu.VMEM((CHUNKS, KEYS, 256), f32),
            pltpu.VMEM((24, 8, 128), f32),
            pltpu.VMEM((8, 512), f32),
            pltpu.VMEM((CHUNKS, 2, 2, STRIP, 128), bf16),
            pltpu.VMEM((CHUNKS, 2, 2, STRIP, 128), bf16),
            pltpu.VMEM((CHUNKS, 2, CENTRE, 128), f32),
            pltpu.VMEM((CHUNKS, 2, 2, SIDE, 128), bf16),
            pltpu.VMEM((CHUNKS, 2, 2, SIDE, 128), bf16),
        ]
        + semaphores,
        compiler_params=pltpu.CompilerParams(
            collective_id=0, has_side_effects=True, vmem_limit_bytes=40 * 1024 * 1024
        ),
        name="neighbourhood",
    )(*flat, rel_bias)
    return tuple(x.reshape(height, breadth, channels) for x in found)


def solution(mesh):
    tiled = P("lat", "lon", None)
    return jax.shard_map(
        shards, mesh=mesh, in_specs=(tiled,) * 4 + (P(),), out_specs=(tiled,) * 4, check_vma=False
    )
```

time: 277 us -> 84.9 us (0.31)
  the two profiles are of different devices: /device:TPU:72 before, /device:TPU:65 now
where the time goes in v1:
time: 84.9 us; the launch traced here: 84.7 us
  Pallas kernels  77.1 us (91%)
  local copies, waits for them, and re-layouts  6.93 us (8%)
    pallas_call x1, Pallas kernels, shards(): pl.pallas_call(kernel, out_shape=[jax.ShapeDtypeStruct((height * breadth,...  77.1 us
    unnamed x14, local copies, waits for them, and re-layouts  6.93 us

profile of v1, /device:TPU:65, one launch (start us, length us, event | category | flops | bytes accessed | tf_op | source)
XLA Modules:
  0.0 84.7 jit_solution(4589015776492562987)
XLA Ops:
  0.6 0.0 copy-start
  0.6 0.9 %copy-done = bf16[8,16,512]{2,1,0:T(8,128)(2,1)S(1)} copy-done((bf16[8,16,512]{2,1,0:T(8,128)(2,1)S(1)}, bf16[8,16,512]{2,1,0:T(8,128)(2,1)}, u32[]{:S(2)}) %copy-start) | copy-done | bytes 131096
  1.5 0.0 copy-start.1
  1.5 0.9 %copy-done.1 = bf16[8,16,512]{2,1,0:T(8,128)(2,1)S(1)} copy-done((bf16[8,16,512]{2,1,0:T(8,128)(2,1)S(1)}, bf16[8,16,512]{2,1,0:T(8,128)(2,1)}, u32[]{:S(2)}) %copy-start.1) | copy-done | bytes 131096
  2.4 0.0 copy-start.2
  2.4 0.9 %copy-done.2 = bf16[8,16,512]{2,1,0:T(8,128)(2,1)S(1)} copy-done((bf16[8,16,512]{2,1,0:T(8,128)(2,1)S(1)}, bf16[8,16,512]{2,1,0:T(8,128)(2,1)}, u32[]{:S(2)}) %copy-start.2) | copy-done | bytes 131096
  3.3 0.0 copy-start.3
  3.3 0.9 %copy-done.3 = bf16[8,16,512]{2,1,0:T(8,128)(2,1)S(1)} copy-done((bf16[8,16,512]{2,1,0:T(8,128)(2,1)S(1)}, bf16[8,16,512]{2,1,0:T(8,128)(2,1)}, u32[]{:S(2)}) %copy-start.3) | copy-done | bytes 131096
  4.3 0.0 copy-start.4
  4.3 0.7 copy-done.4
  4.9 77.1 %neighbourhood.1 = (bf16[128,512]{1,0:T(8,128)(2,1)S(1)}, bf16[128,512]{1,0:T(8,128)(2,1)S(1)}, bf16[128,512]{1,0:T(8,128)(2,1)S(1)}, bf16[128,512]{1,0:T(8,128)(2,1)S(1)}) custom-call(bf16[128,512]{1,0:T(8,128)(2,1)S(1)} %bitcast.12, bf16[128,512]{1,0:T(8,128)(2,1)S(1)} %bitcast.13, bf16[128,512]{1,0:T(8,128)(2,1)S(1)} %bitcast.14, ...), custom_call_target="tpu_custom_call" | custom-call | tf_op jit(solution)/shard_map/neighbourhood/pallas_call | solution.py:341
  82.1 0.7 copy.13
  82.7 0.7 copy.14
  83.4 0.7 copy.15
  84.0 0.7 copy.16
Async XLA Ops:
  0.6 0.9 %copy-start = (bf16[8,16,512]{2,1,0:T(8,128)(2,1)S(1)}, bf16[8,16,512]{2,1,0:T(8,128)(2,1)}, u32[]{:S(2)}) copy-start(bf16[8,16,512]{2,1,0:T(8,128)(2,1)} %param.5) | copy-start | bytes 393220
  1.5 0.9 %copy-start.1 = (bf16[8,16,512]{2,1,0:T(8,128)(2,1)S(1)}, bf16[8,16,512]{2,1,0:T(8,128)(2,1)}, u32[]{:S(2)}) copy-start(bf16[8,16,512]{2,1,0:T(8,128)(2,1)} %param.6) | copy-start | bytes 393220
  2.4 0.9 %copy-start.2 = (bf16[8,16,512]{2,1,0:T(8,128)(2,1)S(1)}, bf16[8,16,512]{2,1,0:T(8,128)(2,1)}, u32[]{:S(2)}) copy-start(bf16[8,16,512]{2,1,0:T(8,128)(2,1)} %param.7) | copy-start | bytes 393220
  3.3 0.9 %copy-start.3 = (bf16[8,16,512]{2,1,0:T(8,128)(2,1)S(1)}, bf16[8,16,512]{2,1,0:T(8,128)(2,1)}, u32[]{:S(2)}) copy-start(bf16[8,16,512]{2,1,0:T(8,128)(2,1)} %param.8) | copy-start | bytes 393220
  4.3 0.7 copy-start.4

commit v2 on v1

--- a/solution.py
+++ b/solution.py
@@ -10,19 +10,20 @@
 SPAN = 13
 MESH = pl.DeviceIdType.MESH
 NEG = -1e30
+LIMIT = 56 * 1000 * 1000
 
 CHUNKS = 4
 HEIGHT = 8
 BREADTH = 16
 SIDE = 48
-WEST = 96
-EAST = 144
+OWN = 96
+WEST = 128
+EAST = 176
 CENTRE = 224
 STRIP = 192
 NORTH = CENTRE
 SOUTH = CENTRE + STRIP
 KEYS = CENTRE + 2 * STRIP
-ROW_AT = [0, 16, 32, 48, 64, 80, 192, 208]
 
 
 def side_groups(base, kind):
@@ -37,8 +38,8 @@
     def sides(base):
         return side_groups(base, 2) + side_groups(base, 5)
 
-    centre = row_groups(0, range(6)) + sides(0) + row_groups(0, (6, 7))
-    north = row_groups(-8, range(2, 6)) + sides(-8) + row_groups(-8, (6, 7))
+    centre = row_groups(0, range(8)) + sides(0)
+    north = row_groups(-8, range(2, 8)) + sides(-8)
     south = row_groups(8, range(6)) + sides(8)
     return [(g, 0) for g in centre] + [(g, 1) for g in north] + [(g, 2) for g in south]
 
@@ -67,9 +68,9 @@
 
 
 def kernel(
-    q_ref, k_ref, v_ref, g_ref, rel_ref, o_ref, dq_ref, dk_ref, dv_ref,
-    cells, edges, bias, table, padded, strips_out, strips_in, centre, sides_out, sides_in,
-    lon_s, lon_r, lat_s, lat_r, rlat_s, rlat_r, rlon_s, rlon_r,
+    q_hbm, k_hbm, v_hbm, g_hbm, rel_hbm, o_hbm, dq_hbm, dk_hbm, dv_hbm,
+    o_ref, dq_ref, dk_ref, dv_ref, q_ref, k_ref, v_ref, g_ref, rel_ref, cells, edges, bias, table, padded, strips_out, strips_in, centre, sides_out, sides_in,
+    lon_s, lon_r, lat_s, lat_r, rlat_s, rlat_r, rlon_s, rlon_r, own_s, own_r, load_s, store_s,
 ):
     lat, lon = lax.axis_index("lat"), lax.axis_index("lon")
     n_lat, n_lon = lax.axis_size("lat"), lax.axis_size("lon")
@@ -93,14 +94,32 @@
     def _():
         pl.semaphore_signal(barrier, inc=1, device_id=south, device_id_type=MESH)
 
+    loads = [
+        pltpu.make_async_copy(src, dst, load_s.at[i])
+        for i, (src, dst) in enumerate(
+            [(k_hbm, k_ref), (v_hbm, v_ref), (rel_hbm, rel_ref), (q_hbm, q_ref), (g_hbm, g_ref)]
+        )
+    ]
+    for load in loads:
+        load.start()
+
     def lanes(g):
         return pl.ds(128 * g, 128)
 
+    def stores(g, which):
+        pairs = [(o_ref, o_hbm), (dq_ref, dq_hbm), (dk_ref, dk_hbm), (dv_ref, dv_hbm)]
+        return [
+            pltpu.make_async_copy(pairs[i][0].at[:, lanes(g)], pairs[i][1].at[:, lanes(g)], store_s.at[i, g])
+            for i in which
+        ]
+
+    for load in loads[:2]:
+        load.wait()
+
     for g in range(CHUNKS):
         for a, ref in ((0, k_ref), (1, v_ref)):
             block = ref[:, lanes(g)]
-            cells[g, a, 0:96] = block[0:96]
-            cells[g, a, 192:224] = block[96:128]
+            cells[g, a, 0:128] = block
             wide = block.astype(jnp.float32)
             low = [wide[16 * r : 16 * r + 8] for r in range(8)]
             high = [wide[16 * r + 8 : 16 * r + 16] for r in range(8)]
@@ -128,19 +147,30 @@
             remote(edges.at[g, 1], cells.at[g, :, pl.ds(WEST, SIDE)], lon_s, lon_r, g, 1, east),
         ]
 
+    def own_copies():
+        up = remote(cells.at[:, :, pl.ds(0, OWN)], cells.at[:, :, pl.ds(SOUTH, OWN)], own_s, own_r, 0, 0, north)
+        down = remote(cells.at[:, :, pl.ds(32, OWN)], cells.at[:, :, pl.ds(NORTH, OWN)], own_s, own_r, 0, 1, south)
+        return up, down
+
     def lat_copies(g):
-        up = remote(
-            cells.at[g, :, pl.ds(0, STRIP)], cells.at[g, :, pl.ds(SOUTH, STRIP)], lat_s, lat_r, g, 0, north
-        )
-        down = remote(
-            cells.at[g, :, pl.ds(32, STRIP)], cells.at[g, :, pl.ds(NORTH, STRIP)], lat_s, lat_r, g, 1, south
-        )
+        sides = cells.at[g, :, pl.ds(WEST, 2 * SIDE)]
+        up = remote(sides, cells.at[g, :, pl.ds(SOUTH + OWN, 2 * SIDE)], lat_s, lat_r, g, 0, north)
+        down = remote(sides, cells.at[g, :, pl.ds(NORTH + OWN, 2 * SIDE)], lat_s, lat_r, g, 1, south)
         return up, down
 
     def back_lat_copies(g):
-        up = remote(strips_out.at[g, 0], strips_in.at[g, 0], rlat_s, rlat_r, g, 0, north)
-        down = remote(strips_out.at[g, 1], strips_in.at[g, 1], rlat_s, rlat_r, g, 1, south)
-        return up, down
+        def copy(way, target):
+            part = pl.ds(OWN, 2 * SIDE)
+            return remote(strips_out.at[way, g, :, part], strips_in.at[way, g, :, part], rlat_s, rlat_r, g, way, target)
+
+        return copy(0, north), copy(1, south)
+
+    def back_own_copies():
+        def copy(way, target):
+            part = pl.ds(0, OWN)
+            return remote(strips_out.at[way, :, :, part], strips_in.at[way, :, :, part], own_s, own_r, 1, way, target)
+
+        return copy(0, north), copy(1, south)
 
     def back_lon_copies(g):
         return [
@@ -173,6 +203,7 @@
     for g in range(CHUNKS):
         for copy in lon_copies(g):
             copy.start()
+    start_pair(own_copies())
 
     for g in range(CHUNKS):
 
@@ -183,6 +214,9 @@
         @pl.when(jnp.logical_not(has_south))
         def _():
             cells[g, :, SOUTH : SOUTH + STRIP] = jnp.zeros((2, STRIP, 128), jnp.bfloat16)
+
+    for load in loads[2:]:
+        load.wait()
 
     padded[...] = jnp.full(padded.shape, NEG, jnp.float32)
     padded[:, 128 : 128 + SPAN * SPAN] = rel_ref[...]
@@ -251,13 +285,15 @@
         grad_v = dot(weights, grads, 1, 0)
         grad_k = dot(dscore, queries, 1, 0) * factor
         for a, found in ((0, grad_k), (1, grad_v)):
-            strips_out[g, 0, a] = found[NORTH : NORTH + STRIP].astype(jnp.bfloat16)
-            strips_out[g, 1, a] = found[SOUTH : SOUTH + STRIP].astype(jnp.bfloat16)
+            strips_out[0, g, a] = found[NORTH : NORTH + STRIP].astype(jnp.bfloat16)
+            strips_out[1, g, a] = found[SOUTH : SOUTH + STRIP].astype(jnp.bfloat16)
             centre[g, a] = found[:CENTRE]
         start_pair(back_lat_copies(g))
         o_ref[:, lanes(g)] = from_heads(dot(values, weights, 0, 0)).astype(jnp.bfloat16)
         grad_q = from_heads(dot(keys, dscore, 0, 0)) * factor
         dq_ref[:, lanes(g)] = grad_q.astype(jnp.bfloat16)
+        for store in stores(g, (0, 1)):
+            store.start()
 
     def return_sides(g):
         wait_pair(back_lat_copies(g))
@@ -265,12 +301,12 @@
         @pl.when(has_south)
         def _():
             for a in range(2):
-                centre[g, a, 32:224] += strips_in[g, 0, a].astype(jnp.float32)
+                centre[g, a, WEST:CENTRE] += strips_in[0, g, a, OWN:STRIP].astype(jnp.float32)
 
         @pl.when(has_north)
         def _():
             for a in range(2):
-                centre[g, a, 0:192] += strips_in[g, 1, a].astype(jnp.float32)
+                centre[g, a, WEST:CENTRE] += strips_in[1, g, a, OWN:STRIP].astype(jnp.float32)
 
         for a in range(2):
             sides_out[g, 0, a] = centre[g, a, WEST : WEST + SIDE].astype(jnp.bfloat16)
@@ -298,69 +334,116 @@
                     high = jnp.where(
                         slot < 4, pltpu.roll(e[0], 4, 0), jnp.where(slot < 6, pltpu.roll(e[1], 6, 0), e[2])
                     )
-                at = ROW_AT[r]
+                at = 16 * r
                 rows.append(centre[g, a, at : at + 8] + jnp.where(slot < 6, low, 0.0))
                 rows.append(centre[g, a, at + 8 : at + 16] + jnp.where(slot >= 2, high, 0.0))
             ref[:, lanes(g)] = jnp.concatenate(rows, axis=0).astype(jnp.bfloat16)
-
+        for store in stores(g, (2, 3)):
+            store.start()
+
+    wait_pair(own_copies())
     forward_strips(0)
     forward_strips(1)
+    forward_strips(2)
     attend(0)
-    forward_strips(2)
-    return_sides(0)
-    attend(1)
     forward_strips(3)
-    return_sides(1)
-    attend(2)
-    return_sides(2)
-    attend(3)
-    return_sides(3)
+    for g in range(1, CHUNKS):
+        attend(g)
+    start_pair(back_own_copies())
+    for g in range(CHUNKS):
+        return_sides(g)
+
+    wait_pair(back_own_copies())
+
+    @pl.when(has_south)
+    def _():
+        for g in range(CHUNKS):
+            for a in range(2):
+                centre[g, a, 32:128] += strips_in[0, g, a, 0:OWN].astype(jnp.float32)
+
+    @pl.when(has_north)
+    def _():
+        for g in range(CHUNKS):
+            for a in range(2):
+                centre[g, a, 0:96] += strips_in[1, g, a, 0:OWN].astype(jnp.float32)
+
     for g in range(CHUNKS):
         finish(g)
 
+    def wait_sent(copies):
+        up, down = copies
+
+        @pl.when(has_north)
+        def _():
+            up.wait_send()
+
+        @pl.when(has_south)
+        def _():
+            down.wait_send()
+
+    wait_sent(own_copies())
+    wait_sent(back_own_copies())
     for g in range(CHUNKS):
         for copy in lon_copies(g) + back_lon_copies(g):
             copy.wait_send()
-        for up, down in (lat_copies(g), back_lat_copies(g)):
-
-            @pl.when(has_north)
-            def _():
-                up.wait_send()
-
-            @pl.when(has_south)
-            def _():
-                down.wait_send()
+        wait_sent(lat_copies(g))
+        wait_sent(back_lat_copies(g))
+        for store in stores(g, range(4)):
+            store.wait()
+
+
+def write(*refs):
+    sources, targets, sems = refs[:4], refs[4:8], refs[8]
+    copies = [pltpu.make_async_copy(s, t, sems.at[i]) for i, (s, t) in enumerate(zip(sources, targets))]
+    for copy in copies:
+        copy.start()
+    for copy in copies:
+        copy.wait()
 
 
 def shards(queries, key_cells, value_cells, grad_output, rel_bias):
     height, breadth, channels = queries.shape
-    flat = [x.reshape(height * breadth, channels) for x in (queries, key_cells, value_cells, grad_output)]
+    count = height * breadth
+    flat = [x.reshape(count, channels) for x in (queries, key_cells, value_cells, grad_output)]
     bf16, f32 = jnp.bfloat16, jnp.float32
-    vmem = pl.BlockSpec(memory_space=pltpu.VMEM)
-    semaphores = [pltpu.SemaphoreType.DMA((CHUNKS, 2))] * 8
+    hbm = pl.BlockSpec(memory_space=pltpu.HBM)
+    shapes = [jax.ShapeDtypeStruct((count, channels), bf16)] * 4
     found = pl.pallas_call(
         kernel,
-        out_shape=[jax.ShapeDtypeStruct((height * breadth, channels), bf16)] * 4,
-        in_specs=[vmem] * 5,
-        out_specs=[vmem] * 4,
-        scratch_shapes=[
+        out_shape=shapes,
+        in_specs=[hbm] * 5,
+        out_specs=[hbm] * 4,
+        scratch_shapes=[pltpu.VMEM((count, channels), bf16)] * 8
+        + [
+            pltpu.VMEM(rel_bias.shape, f32),
             pltpu.VMEM((CHUNKS, 2, KEYS, 128), bf16),
             pltpu.VMEM((CHUNKS, 2, 2, SIDE, 128), bf16),
             pltpu.VMEM((CHUNKS, KEYS, 256), f32),
             pltpu.VMEM((24, 8, 128), f32),
             pltpu.VMEM((8, 512), f32),
-            pltpu.VMEM((CHUNKS, 2, 2, STRIP, 128), bf16),
-            pltpu.VMEM((CHUNKS, 2, 2, STRIP, 128), bf16),
+            pltpu.VMEM((2, CHUNKS, 2, STRIP, 128), bf16),
+            pltpu.VMEM((2, CHUNKS, 2, STRIP, 128), bf16),
             pltpu.VMEM((CHUNKS, 2, CENTRE, 128), f32),
             pltpu.VMEM((CHUNKS, 2, 2, SIDE, 128), bf16),
             pltpu.VMEM((CHUNKS, 2, 2, SIDE, 128), bf16),
         ]
-        + semaphores,
+        + [pltpu.SemaphoreType.DMA((CHUNKS, 2))] * 8
+        + [pltpu.SemaphoreType.DMA((2, 2))] * 2
+        + [pltpu.SemaphoreType.DMA((5,)), pltpu.SemaphoreType.DMA((4, CHUNKS))],
         compiler_params=pltpu.CompilerParams(
-            collective_id=0, has_side_effects=True, vmem_limit_bytes=40 * 1024 * 1024
+            collective_id=0, has_side_effects=True, vmem_limit_bytes=LIMIT
         ),
         name="neighbourhood",
     )(*flat, rel_bias)
+    found = pl.pallas_call(
+        write,
+        out_shape=shapes,
+        in_specs=[hbm] * 4,
+        out_specs=[hbm] * 4,
+        scratch_shapes=[pltpu.SemaphoreType.DMA((4,))],
+        compiler_params=pltpu.CompilerParams(vmem_limit_bytes=LIMIT),
+        name="write",
+    )(*found)
     return tuple(x.reshape(height, breadth, channels) for x in found)
 
 

time: 84.9 us -> 77.1 us (0.908)
  local copies, waits for them, and re-layouts: 6.93 us -> 0.69 us
  Pallas kernels: 77.1 us -> 75.6 us
    unnamed x14 -> x2, local copies, waits for them, and re-layouts: 6.93 us -> 0.69 us
    pallas_call x1 -> x2, Pallas kernels: 77.1 us -> 75.6 us  [the longest x1 74.8 us: shards(): pl.pallas_call(kernel, out_shape=shapes, in_specs=[hbm] * 5, out_specs=[h...]
where the time goes in v2:
time: 77.1 us; the launch traced here: 76.9 us
  Pallas kernels  75.6 us (98%)
    pallas_call x1, Pallas kernels, shards(): pl.pallas_call(kernel, out_shape=shapes, in_specs=[hbm] * 5, out_specs=[h...  74.8 us

profile of v2, /device:TPU:65, one launch (start us, length us, event | category | flops | bytes accessed | tf_op | source)
XLA Modules:
  0.0 76.9 jit_solution(14928194736069225107)
XLA Ops:
  0.6 0.0 copy-start
  0.6 0.7 copy-done
  1.3 74.8 %neighbourhood.1 = (bf16[128,512]{1,0:T(8,128)(2,1)S(1)}, bf16[128,512]{1,0:T(8,128)(2,1)S(1)}, bf16[128,512]{1,0:T(8,128)(2,1)S(1)}, bf16[128,512]{1,0:T(8,128)(2,1)S(1)}) custom-call(bf16[128,512]{1,0:T(8,128)(2,1)} %bitcast.8, bf16[128,512]{1,0:T(8,128)(2,1)} %bitcast.9, bf16[128,512]{1,0:T(8,128)(2,1)} %bitcast.10, bf16[128,512]{1,0:T(8,128)(2,1)} %bitcast.11, ...), custom_call_target="tpu_custom_call" | custom-call | tf_op jit(solution)/shard_map/neighbourhood/pallas_call | solution.py:411
  76.1 0.8 %write.1 = (bf16[128,512]{1,0:T(8,128)(2,1)}, bf16[128,512]{1,0:T(8,128)(2,1)}, bf16[128,512]{1,0:T(8,128)(2,1)}, bf16[128,512]{1,0:T(8,128)(2,1)}) custom-call(bf16[128,512]{1,0:T(8,128)(2,1)S(1)} %get-tuple-element.12.refs_0_, bf16[128,512]{1,0:T(8,128)(2,1)S(1)} %get-tuple-element.13.refs_1_, bf16[128,512]{1,0:T(8,128)(2,1)S(1)} %get-tuple-element.14.refs_2_, ...), custom_call_target="tpu_custom_call" | custom-call | tf_op jit(solution)/shard_map/write/pallas_call | solution.py:438
Async XLA Ops:
  0.6 0.7 copy-start

commit v3 on v2

--- a/solution.py
+++ b/solution.py
@@ -10,7 +10,7 @@
 SPAN = 13
 MESH = pl.DeviceIdType.MESH
 NEG = -1e30
-LIMIT = 56 * 1000 * 1000
+LIMIT = 40 * 1024 * 1024
 
 CHUNKS = 4
 HEIGHT = 8
@@ -68,9 +68,9 @@
 
 
 def kernel(
-    q_hbm, k_hbm, v_hbm, g_hbm, rel_hbm, o_hbm, dq_hbm, dk_hbm, dv_hbm,
-    o_ref, dq_ref, dk_ref, dv_ref, q_ref, k_ref, v_ref, g_ref, rel_ref, cells, edges, bias, table, padded, strips_out, strips_in, centre, sides_out, sides_in,
-    lon_s, lon_r, lat_s, lat_r, rlat_s, rlat_r, rlon_s, rlon_r, own_s, own_r, load_s, store_s,
+    q_hbm, k_hbm, v_hbm, g_hbm, rel_hbm, o_ref, dq_ref, dk_ref, dv_ref,
+    q_ref, k_ref, v_ref, g_ref, rel_ref, cells, edges, bias, table, padded, strips_out, strips_in, centre, sides_out, sides_in,
+    kept, lon_s, lon_r, lat_s, lat_r, rlat_s, rlat_r, rlon_s, rlon_r, own_s, own_r, load_s,
 ):
     lat, lon = lax.axis_index("lat"), lax.axis_index("lon")
     n_lat, n_lon = lax.axis_size("lat"), lax.axis_size("lon")
@@ -105,13 +105,6 @@
 
     def lanes(g):
         return pl.ds(128 * g, 128)
-
-    def stores(g, which):
-        pairs = [(o_ref, o_hbm), (dq_ref, dq_hbm), (dk_ref, dk_hbm), (dv_ref, dv_hbm)]
-        return [
-            pltpu.make_async_copy(pairs[i][0].at[:, lanes(g)], pairs[i][1].at[:, lanes(g)], store_s.at[i, g])
-            for i in which
-        ]
 
     for load in loads[:2]:
         load.wait()
@@ -289,11 +282,13 @@
             strips_out[1, g, a] = found[SOUTH : SOUTH + STRIP].astype(jnp.bfloat16)
             centre[g, a] = found[:CENTRE]
         start_pair(back_lat_copies(g))
-        o_ref[:, lanes(g)] = from_heads(dot(values, weights, 0, 0)).astype(jnp.bfloat16)
-        grad_q = from_heads(dot(keys, dscore, 0, 0)) * factor
+        kept[g, 0] = weights
+        kept[g, 1] = dscore
+
+    def outputs(g):
+        o_ref[:, lanes(g)] = from_heads(dot(cells[g, 1], kept[g, 0], 0, 0)).astype(jnp.bfloat16)
+        grad_q = from_heads(dot(cells[g, 0], kept[g, 1], 0, 0)) * factor
         dq_ref[:, lanes(g)] = grad_q.astype(jnp.bfloat16)
-        for store in stores(g, (0, 1)):
-            store.start()
 
     def return_sides(g):
         wait_pair(back_lat_copies(g))
@@ -338,20 +333,23 @@
                 rows.append(centre[g, a, at : at + 8] + jnp.where(slot < 6, low, 0.0))
                 rows.append(centre[g, a, at + 8 : at + 16] + jnp.where(slot >= 2, high, 0.0))
             ref[:, lanes(g)] = jnp.concatenate(rows, axis=0).astype(jnp.bfloat16)
-        for store in stores(g, (2, 3)):
-            store.start()
 
     wait_pair(own_copies())
     forward_strips(0)
     forward_strips(1)
     forward_strips(2)
+    forward_strips(3)
     attend(0)
-    forward_strips(3)
-    for g in range(1, CHUNKS):
-        attend(g)
+    attend(1)
+    attend(2)
+    return_sides(0)
+    attend(3)
+    return_sides(1)
+    return_sides(2)
+    return_sides(3)
     start_pair(back_own_copies())
     for g in range(CHUNKS):
-        return_sides(g)
+        outputs(g)
 
     wait_pair(back_own_copies())
 
@@ -388,8 +386,6 @@
             copy.wait_send()
         wait_sent(lat_copies(g))
         wait_sent(back_lat_copies(g))
-        for store in stores(g, range(4)):
-            store.wait()
 
 
 def write(*refs):
@@ -412,8 +408,8 @@
         kernel,
         out_shape=shapes,
         in_specs=[hbm] * 5,
-        out_specs=[hbm] * 4,
-        scratch_shapes=[pltpu.VMEM((count, channels), bf16)] * 8
+        out_specs=[pl.BlockSpec(memory_space=pltpu.VMEM)] * 4,
+        scratch_shapes=[pltpu.VMEM((count, channels), bf16)] * 4
         + [
             pltpu.VMEM(rel_bias.shape, f32),
             pltpu.VMEM((CHUNKS, 2, KEYS, 128), bf16),
@@ -426,15 +422,16 @@
             pltpu.VMEM((CHUNKS, 2, CENTRE, 128), f32),
             pltpu.VMEM((CHUNKS, 2, 2, SIDE, 128), bf16),
             pltpu.VMEM((CHUNKS, 2, 2, SIDE, 128), bf16),
+            pltpu.VMEM((CHUNKS, 2, KEYS, 256), bf16),
         ]
         + [pltpu.SemaphoreType.DMA((CHUNKS, 2))] * 8
         + [pltpu.SemaphoreType.DMA((2, 2))] * 2
-        + [pltpu.SemaphoreType.DMA((5,)), pltpu.SemaphoreType.DMA((4, CHUNKS))],
+        + [pltpu.SemaphoreType.DMA((5,))],
         compiler_params=pltpu.CompilerParams(
             collective_id=0, has_side_effects=True, vmem_limit_bytes=LIMIT
         ),
         name="neighbourhood",
-    )(*flat, rel_bias)
+    )(*[pltpu.with_memory_space_constraint(x, pltpu.HBM) for x in flat + [rel_bias]])
     found = pl.pallas_call(
         write,
         out_shape=shapes,

time: 77.1 us -> 72.2 us (0.936)
  the two profiles are of different devices: /device:TPU:65 before, /device:TPU:96 now
where the time goes in v3:
time: 72.2 us; the launch traced here: 72 us
  Pallas kernels  71.4 us (99%)
    pallas_call x1, Pallas kernels, shards(): pl.pallas_call(kernel, out_shape=shapes, in_specs=[hbm] * 5, out_specs=[p...  70.6 us

profile of v3, /device:TPU:96, one launch (start us, length us, event | category | flops | bytes accessed | tf_op | source)
XLA Modules:
  0.0 72.0 jit_solution(1060410257495330495)
XLA Ops:
  0.6 70.6 %neighbourhood.1 = (bf16[128,512]{1,0:T(8,128)(2,1)S(1)}, bf16[128,512]{1,0:T(8,128)(2,1)S(1)}, bf16[128,512]{1,0:T(8,128)(2,1)S(1)}, bf16[128,512]{1,0:T(8,128)(2,1)S(1)}) custom-call(bf16[128,512]{1,0:T(8,128)(2,1)} %bitcast.8, bf16[128,512]{1,0:T(8,128)(2,1)} %bitcast.9, bf16[128,512]{1,0:T(8,128)(2,1)} %bitcast.10, bf16[128,512]{1,0:T(8,128)(2,1)} %bitcast.11, ...), custom_call_target="tpu_custom_call" | custom-call | tf_op jit(solution)/shard_map/neighbourhood/pallas_call | solution.py:407
  71.2 0.8 %write.1 = (bf16[128,512]{1,0:T(8,128)(2,1)}, bf16[128,512]{1,0:T(8,128)(2,1)}, bf16[128,512]{1,0:T(8,128)(2,1)}, bf16[128,512]{1,0:T(8,128)(2,1)}) custom-call(bf16[128,512]{1,0:T(8,128)(2,1)S(1)} %get-tuple-element.12.refs_0_, bf16[128,512]{1,0:T(8,128)(2,1)S(1)} %get-tuple-element.13.refs_1_, bf16[128,512]{1,0:T(8,128)(2,1)S(1)} %get-tuple-element.14.refs_2_, ...), custom_call_target="tpu_custom_call" | custom-call | tf_op jit(solution)/shard_map/write/pallas_call | solution.py:435

commit v4 on v3

--- a/solution.py
+++ b/solution.py
@@ -390,7 +390,12 @@
 
 def write(*refs):
     sources, targets, sems = refs[:4], refs[4:8], refs[8]
-    copies = [pltpu.make_async_copy(s, t, sems.at[i]) for i, (s, t) in enumerate(zip(sources, targets))]
+    half = sources[0].shape[0] // 2
+    copies = [
+        pltpu.make_async_copy(s.at[pl.ds(half * j, half)], t.at[pl.ds(half * j, half)], sems.at[i, j])
+        for i, (s, t) in enumerate(zip(sources, targets))
+        for j in range(2)
+    ]
     for copy in copies:
         copy.start()
     for copy in copies:
@@ -437,7 +442,7 @@
         out_shape=shapes,
         in_specs=[hbm] * 4,
         out_specs=[hbm] * 4,
-        scratch_shapes=[pltpu.SemaphoreType.DMA((4,))],
+        scratch_shapes=[pltpu.SemaphoreType.DMA((4, 2))],
         compiler_params=pltpu.CompilerParams(vmem_limit_bytes=LIMIT),
         name="write",
     )(*found)

time: 72.2 us -> 72.2 us (level)
  no operation moved by 1% of the time
where the time goes in v4:
time: 72.2 us; the launch traced here: 72.1 us
  Pallas kernels  71.4 us (99%)
    pallas_call x1, Pallas kernels, shards(): pl.pallas_call(kernel, out_shape=shapes, in_specs=[hbm] * 5, out_specs=[p...  70.6 us

profile of v4, /device:TPU:96, one launch (start us, length us, event | category | flops | bytes accessed | tf_op | source)
XLA Modules:
  0.0 72.1 jit_solution(16707811214489344708)
XLA Ops:
  0.6 70.6 %neighbourhood.1 = (bf16[128,512]{1,0:T(8,128)(2,1)S(1)}, bf16[128,512]{1,0:T(8,128)(2,1)S(1)}, bf16[128,512]{1,0:T(8,128)(2,1)S(1)}, bf16[128,512]{1,0:T(8,128)(2,1)S(1)}) custom-call(bf16[128,512]{1,0:T(8,128)(2,1)} %bitcast.8, bf16[128,512]{1,0:T(8,128)(2,1)} %bitcast.9, bf16[128,512]{1,0:T(8,128)(2,1)} %bitcast.10, bf16[128,512]{1,0:T(8,128)(2,1)} %bitcast.11, ...), custom_call_target="tpu_custom_call" | custom-call | tf_op jit(solution)/shard_map/neighbourhood/pallas_call | solution.py:412
  71.2 0.9 %write.1 = (bf16[128,512]{1,0:T(8,128)(2,1)}, bf16[128,512]{1,0:T(8,128)(2,1)}, bf16[128,512]{1,0:T(8,128)(2,1)}, bf16[128,512]{1,0:T(8,128)(2,1)}) custom-call(bf16[128,512]{1,0:T(8,128)(2,1)S(1)} %get-tuple-element.12.refs_0_, bf16[128,512]{1,0:T(8,128)(2,1)S(1)} %get-tuple-element.13.refs_1_, bf16[128,512]{1,0:T(8,128)(2,1)S(1)} %get-tuple-element.14.refs_2_, ...), custom_call_target="tpu_custom_call" | custom-call | tf_op jit(solution)/shard_map/write/pallas_call | solution.py:440
